TPU v7x, 32 devices: a whole 2x2x4 slice. The times are simulated.
32 devices in a mesh: members: 4 (over y, core), space: 8 (over z, x).
Axes of the slice: x: 2, y: 2, z: 4, core: 2. Of those that a mesh axis runs over, the one named last changes fastest.
Arguments:
- ensemble: float32 [3, 512, 64, 256], P(None, 'members', 'space'), may hold values from -6 to 6
- obs_cells: int32 [8, 4, 128], P('space', 'members'), may hold values from 0 to 1535
- obs_values: float32 [8, 4, 128], P('space', 'members'), may hold values from -6 to 6
- obs_var: float32 [8, 4, 128], P('space', 'members'), may hold values from 0.25 to 4
- obs_noise: float32 [512, 8, 4, 128], P(None, 'space', 'members'), may hold values from -6 to 6
- assign: int32 [512], replicated, may hold values from 0 to 511, each once
Outputs:
- analysis: float32 [3, 512, 64, 256], P(None, 'members', 'space')
Inputs may be any that keep to these rules, and one draw needn't show every extreme that they name: assign holds every member once. obs_cells[r, c, k] = field * 8 * 64 + row * 64 + column within tile (r, c); repeats are possible.
All inputs are finite; a program needn't handle non-finite values.
Results may differ from a plain program's by a relative error of at most 0.0003.
Values sent between devices are 32-bit elements; how exact they have to be, the bound alone decides.
A program may use at most 64 MiB of HBM per device.

v0:
```python
import jax
import jax.numpy as jnp
from jax import lax
from jax.sharding import PartitionSpec as P

TILE_W = 64
STEPS = 4
tstep = 0.1
gravity = 1.0
depth = 1.0
coriolis = 0.25
viscosity = 0.5


def extended(cells, sides, width):
    for axis, dim in sides:
        count = lax.axis_size(axis)
        head = lax.slice_in_dim(cells, 0, width, axis=dim)
        tail = lax.slice_in_dim(cells, cells.shape[dim] - width, cells.shape[dim], axis=dim)
        cells = jnp.concatenate(
            [
                lax.ppermute(tail, axis, [(i, (i + 1) % count) for i in range(count)]),
                cells,
                lax.ppermute(head, axis, [((i + 1) % count, i) for i in range(count)]),
            ],
            axis=dim,
        )
    return cells


def centred_x(field):
    return 0.5 * (jnp.roll(field, -1, axis=2) - jnp.roll(field, 1, axis=2))


def height_update(state):
    eta, east, north = (state[0], state[1], state[2])
    column = depth + eta
    flux_x = centred_x(column * east)[:, 1:-1]
    carried = column * north
    flux_y = 0.5 * (carried[:, 2:] - carried[:, :-2])
    return eta[:, 1:-1] - tstep * (flux_x + flux_y)


def momentum_update(eta, east, north):

    def advance(field, extra):
        inner = field[:, 1:-1]
        grad_x = centred_x(field)[:, 1:-1]
        grad_y = 0.5 * (field[:, 2:] - field[:, :-2])
        spread = (
            jnp.roll(field, -1, axis=2)[:, 1:-1]
            + jnp.roll(field, 1, axis=2)[:, 1:-1]
            + field[:, 2:]
            + field[:, :-2]
            - 4.0 * inner
        )
        return inner + tstep * (
            -east[:, 1:-1] * grad_x - north[:, 1:-1] * grad_y + extra + viscosity * spread
        )

    slope_x = centred_x(eta)[:, 1:-1]
    slope_y = 0.5 * (eta[:, 2:] - eta[:, :-2])
    new_east = advance(east, coriolis * north[:, 1:-1] - gravity * slope_x)
    new_north = advance(north, -coriolis * east[:, 1:-1] - gravity * slope_y)
    return (new_east, new_north)


def thin_pad(state):
    return extended(state, (("space", 2),), 1)


def analyse_tile(tile, near):
    count = tile.shape[1]
    spread_all = jnp.transpose(near[:, :, 0], (2, 0, 1, 3)).reshape(count, -1)
    misfit_all = jnp.transpose(near[:, :, 1], (2, 0, 1, 3)).reshape(count, -1)
    gram = jnp.dot(spread_all, spread_all.T, precision=lax.Precision.HIGHEST) / (
        count - 1
    ) + jnp.eye(count, dtype=jnp.float32)
    factor = jnp.linalg.cholesky(gram)
    reduced = jax.scipy.linalg.cho_solve((factor, True), spread_all)
    mixing = jnp.dot(misfit_all, reduced.T, precision=lax.Precision.HIGHEST) / (count - 1)
    anomaly = tile - jnp.mean(tile, axis=1, keepdims=True)
    return tile + jnp.einsum("ij,fjc->fic", mixing, anomaly, precision=lax.Precision.HIGHEST)


def local(ensemble, obs_cells, obs_values, obs_var, obs_noise, assign):
    state = ensemble
    for step in range(STEPS):
        eta_new = height_update(thin_pad(state))
        padded = thin_pad(jnp.stack([eta_new, state[1], state[2]]))
        east, north = momentum_update(padded[0], padded[1], padded[2])
        state = jnp.stack([eta_new, east, north])
    width = TILE_W
    tiles = lax.all_to_all(state, "members", split_axis=3, concat_axis=1, tiled=True)
    count = tiles.shape[1]
    rows_here = tiles.shape[2]
    tile = tiles.reshape(3, count, rows_here * width)
    tile_cells = rows_here * width
    cells = obs_cells.reshape(-1)
    field_of = cells // tile_cells
    cell_of = cells % tile_cells
    shape = (3, tile_cells, cells.shape[0])
    pick = (
        (lax.broadcasted_iota(jnp.int32, shape, 0) == field_of[None, None, :])
        & (lax.broadcasted_iota(jnp.int32, shape, 1) == cell_of[None, None, :])
    ).astype(jnp.float32)
    observed = jnp.einsum("fmc,fco->mo", tile, pick, precision=lax.Precision.HIGHEST)
    scale = 1.0 / jnp.sqrt(obs_var.reshape(-1))
    mean_obs = jnp.mean(observed, axis=0, keepdims=True)
    spread = (observed - mean_obs) * scale
    noise = jnp.take(obs_noise.reshape(count, -1), assign, axis=0)
    misfit = (obs_values.reshape(-1)[None, :] - observed) * scale + noise
    packed = jnp.stack([spread, misfit])[None, None]
    near = extended(packed, (("members", 1), ("space", 0)), 1)
    updated = analyse_tile(tile, near).reshape(3, count, rows_here, width)
    return lax.all_to_all(updated, "members", split_axis=1, concat_axis=3, tiled=True)


def solution(mesh):
    in_specs = (
        P(None, "members", "space", None),
        P("space", "members", None),
        P("space", "members", None),
        P("space", "members", None),
        P(None, "space", "members", None),
        P(),
    )
    out_specs = P(None, "members", "space", None)
    return jax.shard_map(local, mesh=mesh, in_specs=in_specs, out_specs=out_specs, check_vma=False)
```

profile of v0, /device:TPU:0, one launch (start us, length us, event | category | flops | bytes accessed | tf_op | source)
XLA Modules:
  0.0 610.9 jit_solution(4791062386174462947)
XLA Ops:
  3.1 3.0 collective-permute-start
  6.1 3.1 collective-permute-start.1
  9.4 13.6 %collective-permute-done = f32[3,128,1,256]{1,2,3,0:T(1,128)S(1)} collective-permute-done((f32[3,128,1,256]{1,2,3,0:T(1,128)S(1)}, f32[3,128,1,256]{1,2,3,0:T(1,128)S(1)}, u32[]{:S(2)}, u32[]{:S(2)}) %collective-permute-start) | collective-permute-done | bytes 393248 | tf_op jit(solution)/shard_map/ppermute | solution.py:22
  28.7 4.4 collective-permute-start.3
  33.1 11.5 %collective-permute-done.2 = f32[3,128,1,256]{1,2,3,0:T(1,128)S(1)} collective-permute-done((f32[3,128,1,256]{1,2,3,0:T(1,128)S(1)}, f32[3,128,1,256]{1,2,3,0:T(1,128)S(1)}, u32[]{:S(2)}, u32[]{:S(2)}) %collective-permute-start.2) | collective-permute-done | bytes 393248 | tf_op jit(solution)/shard_map/ppermute | solution.py:22
  44.6 3.9 collective-permute-done.3
  55.4 5.0 collective-permute-start.5
  60.4 11.6 %collective-permute-done.4 = f32[3,128,1,256]{1,2,3,0:T(1,128)S(1)} collective-permute-done((f32[3,128,1,256]{1,2,3,0:T(1,128)S(1)}, f32[3,128,1,256]{1,2,3,0:T(1,128)S(1)}, u32[]{:S(2)}, u32[]{:S(2)}) %collective-permute-start.4) | collective-permute-done | bytes 393248 | tf_op jit(solution)/shard_map/ppermute | solution.py:22
  72.0 4.1 collective-permute-done.5
  79.9 4.7 collective-permute-start.7
  84.6 11.7 %collective-permute-done.6 = f32[3,128,1,256]{1,2,3,0:T(1,128)S(1)} collective-permute-done((f32[3,128,1,256]{1,2,3,0:T(1,128)S(1)}, f32[3,128,1,256]{1,2,3,0:T(1,128)S(1)}, u32[]{:S(2)}, u32[]{:S(2)}) %collective-permute-start.6) | collective-permute-done | bytes 393248 | tf_op jit(solution)/shard_map/ppermute | solution.py:22
  96.3 3.7 collective-permute-done.7
  107.2 4.7 collective-permute-start.9
  111.9 11.7 %collective-permute-done.8 = f32[3,128,1,256]{1,2,3,0:T(1,128)S(1)} collective-permute-done((f32[3,128,1,256]{1,2,3,0:T(1,128)S(1)}, f32[3,128,1,256]{1,2,3,0:T(1,128)S(1)}, u32[]{:S(2)}, u32[]{:S(2)}) %collective-permute-start.8) | collective-permute-done | bytes 393248 | tf_op jit(solution)/shard_map/ppermute | solution.py:22
  130.0 5.0 collective-permute-start.11
  135.0 10.5 %collective-permute-done.10 = f32[3,128,1,256]{1,2,3,0:T(1,128)S(1)} collective-permute-done((f32[3,128,1,256]{1,2,3,0:T(1,128)S(1)}, f32[3,128,1,256]{1,2,3,0:T(1,128)S(1)}, u32[]{:S(2)}, u32[]{:S(2)}) %collective-permute-start.10) | collective-permute-done | bytes 393248 | tf_op jit(solution)/shard_map/ppermute | solution.py:22
  145.5 4.6 collective-permute-done.11
  157.3 4.7 collective-permute-start.13
  162.0 12.4 %collective-permute-done.12 = f32[3,128,1,256]{1,2,3,0:T(1,128)S(1)} collective-permute-done((f32[3,128,1,256]{1,2,3,0:T(1,128)S(1)}, f32[3,128,1,256]{1,2,3,0:T(1,128)S(1)}, u32[]{:S(2)}, u32[]{:S(2)}) %collective-permute-start.12) | collective-permute-done | bytes 393248 | tf_op jit(solution)/shard_map/ppermute | solution.py:22
  174.5 2.7 collective-permute-done.13
  181.1 4.9 collective-permute-start.15
  186.0 11.5 %collective-permute-done.14 = f32[3,128,1,256]{1,2,3,0:T(1,128)S(1)} collective-permute-done((f32[3,128,1,256]{1,2,3,0:T(1,128)S(1)}, f32[3,128,1,256]{1,2,3,0:T(1,128)S(1)}, u32[]{:S(2)}, u32[]{:S(2)}) %collective-permute-start.14) | collective-permute-done | bytes 393248 | tf_op jit(solution)/shard_map/ppermute | solution.py:22
  197.5 4.1 collective-permute-done.15
  209.8 3.8 all-to-all-start
  217.2 33.3 %all-to-all-done = f32[3,128,8,256]{1,2,0,3:T(8,128)S(1)} async-done(((f32[3,128,8,256]{1,2,0,3:T(8,128)}), f32[3,128,8,256]{1,2,0,3:T(8,128)S(1)}, u32[]{:S(2)}, u32[]{:S(2)}) %all-to-all-start) | async-done | bytes 3145760 | tf_op jit(solution)/shard_map/all_to_all | solution.py:94
  250.5 3.7 copy.59
  254.2 5.0 reshape.97
  259.2 3.4 fusion.313
  263.4 11.2 %collective-permute-done.17 = f32[1,1,2,512,128]{3,4,2,1,0:T(8,128)S(1)} collective-permute-done((f32[1,1,2,512,128]{3,4,2,1,0:T(8,128)S(1)}, f32[1,1,2,512,128]{3,4,2,1,0:T(8,128)S(1)}, u32[]{:S(2)}, u32[]{:S(2)}) %collective-permute-start.17) | collective-permute-done | bytes 524320 | tf_op jit(solution)/shard_map/ppermute | solution.py:24
  284.9 63.5 %collective-permute-done.19 = f32[1,3,2,512,128]{3,4,2,1,0:T(8,128)} collective-permute-done((f32[1,3,2,512,128]{3,4,2,1,0:T(8,128)}, f32[1,3,2,512,128]{3,4,2,1,0:T(8,128)}, u32[]{:S(2)}, u32[]{:S(2)}) %collective-permute-start.19) | collective-permute-done | bytes 1572896 | tf_op jit(solution)/shard_map/ppermute | solution.py:24
  350.8 5.7 convert_add_fusion
  363.9 11.7 %cholesky.104 = f32[128,128]{1,0:T(8,128)S(1)} custom-call(f32[128,128]{1,0:T(8,128)S(1)} %cholesky.266), custom_call_target="Cholesky" | custom-call | tf_op jit(solution)/shard_map/jit(cholesky)/cholesky | solution.py:79
  381.1 10.2 %custom-call.34 = f32[1,128,128]{1,2,0:T(8,128)S(1)} custom-call(f32[1,128,128]{2,1,0:T(8,128)S(1)} %get-tuple-element.140), custom_call_target="InvertDiagBlocksLowerTriangular" | custom-call | tf_op jit(solution)/shard_map/jit(cholesky)/cholesky | solution.py:79
  396.2 11.7 %cholesky.217 = f32[128,128]{1,0:T(8,128)S(1)} custom-call(f32[128,128]{1,0:T(8,128)S(1)} %cholesky.270), custom_call_target="Cholesky" | custom-call | tf_op jit(solution)/shard_map/jit(cholesky)/cholesky | solution.py:79
  408.6 9.8 %custom-call.35 = f32[1,128,128]{1,2,0:T(8,128)S(1)} custom-call(f32[1,128,128]{2,1,0:T(8,128)S(1)} %get-tuple-element.137), custom_call_target="InvertDiagBlocksLowerTriangular" | custom-call | tf_op jit(solution)/shard_map/jit(cholesky)/cholesky | solution.py:79
  419.1 11.7 %cholesky.238 = f32[128,128]{1,0:T(8,128)S(1)} custom-call(f32[128,128]{1,0:T(8,128)S(1)} %cholesky.275), custom_call_target="Cholesky" | custom-call | tf_op jit(solution)/shard_map/jit(cholesky)/cholesky | solution.py:79
  431.6 9.9 %custom-call.36 = f32[1,128,128]{1,2,0:T(8,128)S(1)} custom-call(f32[1,128,128]{2,1,0:T(8,128)S(1)} %get-tuple-element.134), custom_call_target="InvertDiagBlocksLowerTriangular" | custom-call | tf_op jit(solution)/shard_map/jit(cholesky)/cholesky | solution.py:79
  442.1 11.7 %cholesky.255 = f32[128,128]{1,0:T(8,128)S(1)} custom-call(f32[128,128]{1,0:T(8,128)S(1)} %convolution_subtract_fusion.8), custom_call_target="Cholesky" | custom-call | tf_op jit(solution)/shard_map/jit(cholesky)/cholesky | solution.py:79
  457.1 10.6 %while.1 = (s32[]{:T(128)}, f32[512,512]{1,0:T(8,128)S(1)}, s32[4,2]{0,1:T(2,128)S(1)}, f32[4,128,128]{2,1,0:T(8,128)}, s32[]{:T(128)}) while((s32[]{:T(128)}, f32[512,512]{1,0:T(8,128)S(1)}, s32[4,2]{0,1:T(2,128)S(1)}, f32[4,128,128]{2,1,0:T(8,128)}, s32[]{:T(128)}) %tuple.90), condition=%wide.while_cond, body=%wide.while_body.sunk | while | flops 2 | bytes 132205 | solution.py:80
  467.7 40.3 %custom-call.37 = f32[4,128,128]{1,2,0:T(8,128)S(1)} custom-call(f32[4,128,128]{2,1,0:T(8,128)} %get-tuple-element.12), custom_call_target="InvertDiagBlocksLowerTriangular" | custom-call | tf_op jit(solution)/shard_map/jit(_cho_solve)/triangular_solve | solution.py:80
  519.1 4.8 fusion.49
  523.9 5.4 bitcast_add_fusion
  529.3 4.2 copy.71
  533.5 7.0 %reshape.132 = f32[4,1,196608]{2,1,0:T(1,128)} reshape(f32[512,3,8,64]{3,2,1,0:T(8,128)} %bitcast.224) | data formatting | bytes 6291456
  540.6 40.7 %all_to_all.33 = f32[4,1,196608]{2,1,0:T(1,128)S(1)} all-to-all(f32[4,1,196608]{2,1,0:T(1,128)} %reshape.132), channel_id=1, replica_groups=mesh['members'=4,'space'=8] {'members'}, dimensions={0} | all-to-all | bytes 6291456 | tf_op jit(solution)/shard_map/all_to_all | solution.py:116
  581.9 10.6 %reduce.25 = f32[4,196608]{1,0:T(4,128)} reduce(f32[4,1,196608]{2,1,0:T(1,128)S(1)} %all_to_all.33, f32[]{:T(128)} %broadcast.379), dimensions={1}, to_apply=%all_to_all.27.reduce_sub_computation | reduce | bytes 6291460 | tf_op jit(solution)/shard_map/all_to_all | solution.py:116
  592.5 7.4 %reshape.133 = f32[512,3,8,64]{3,2,1,0:T(8,128)} reshape(f32[4,196608]{1,0:T(4,128)} %reduce.25) | data formatting | bytes 6291456
  599.9 6.1 %copy.84 = f32[3,4,128,8,64]{2,1,4,3,0:T(4,128)} copy(f32[3,4,128,8,64]{4,3,0,2,1:T(8,128)} %bitcast.225) | data formatting | bytes 6291456 | tf_op jit(solution)/shard_map/all_to_all | solution.py:116
  (208 shorter events, 116.8 us)
Async XLA Ops:
  0.0 213.7 %copy-start = (f32[512,1,1,128]{3,2,1,0:T(1,128)S(1)}, f32[512,1,1,128]{3,2,1,0:T(1,128)}, u32[]{:S(2)}) copy-start(f32[512,1,1,128]{3,2,1,0:T(1,128)} %param.10) | copy-start | bytes 786436
  3.1 19.8 %collective-permute-start = (f32[3,128,1,256]{1,2,3,0:T(1,128)S(1)}, f32[3,128,1,256]{1,2,3,0:T(1,128)S(1)}, u32[]{:S(2)}, u32[]{:S(2)}) collective-permute-start(f32[3,128,1,256]{1,2,3,0:T(1,128)S(1)} %get-tuple-element.59), channel_id=1, source_target_pairs={{0,1},{1,2},{2,3},{3,4},{4,5},{5,6},{6,7},{7,0},{8,9},{9,10},{10,1... | collective-permute-start | bytes 1179656 | tf_op jit(solution)/shard_map/ppermute | solution.py:22
  6.1 19.0 %collective-permute-start.1 = (f32[3,128,1,256]{1,2,3,0:T(1,128)S(1)}, f32[3,128,1,256]{1,2,3,0:T(1,128)S(1)}, u32[]{:S(2)}, u32[]{:S(2)}) collective-permute-start(f32[3,128,1,256]{1,2,3,0:T(1,128)S(1)} %get-tuple-element.60), channel_id=1, source_target_pairs={{1,0},{2,1},{3,2},{4,3},{5,4},{6,5},{7,6},{0,7},{9,8},{10,9},{11,1... | collective-permute-start | bytes 1179656 | tf_op jit(solution)/shard_map/ppermute | solution.py:24
  28.4 16.3 %collective-permute-start.2 = (f32[3,128,1,256]{1,2,3,0:T(1,128)S(1)}, f32[3,128,1,256]{1,2,3,0:T(1,128)S(1)}, u32[]{:S(2)}, u32[]{:S(2)}) collective-permute-start(f32[3,128,1,256]{1,2,3,0:T(1,128)S(1)} %get-tuple-element.57), channel_id=1, source_target_pairs={{0,1},{1,2},{2,3},{3,4},{4,5},{5,6},{6,7},{7,0},{8,9},{9,10},{10,1... | collective-permute-start | bytes 1179656 | tf_op jit(solution)/shard_map/ppermute | solution.py:22
  28.7 19.9 %collective-permute-start.3 = (f32[3,128,1,256]{1,2,3,0:T(1,128)S(1)}, f32[3,128,1,256]{1,2,3,0:T(1,128)S(1)}, u32[]{:S(2)}, u32[]{:S(2)}) collective-permute-start(f32[3,128,1,256]{1,2,3,0:T(1,128)S(1)} %get-tuple-element.58), channel_id=1, source_target_pairs={{1,0},{2,1},{3,2},{4,3},{5,4},{6,5},{7,6},{0,7},{9,8},{10,9},{11,1... | collective-permute-start | bytes 1179656 | tf_op jit(solution)/shard_map/ppermute | solution.py:24
  55.3 16.6 %collective-permute-start.4 = (f32[3,128,1,256]{1,2,3,0:T(1,128)S(1)}, f32[3,128,1,256]{1,2,3,0:T(1,128)S(1)}, u32[]{:S(2)}, u32[]{:S(2)}) collective-permute-start(f32[3,128,1,256]{1,2,3,0:T(1,128)S(1)} %get-tuple-element.55), channel_id=1, source_target_pairs={{0,1},{1,2},{2,3},{3,4},{4,5},{5,6},{6,7},{7,0},{8,9},{9,10},{10,1... | collective-permute-start | bytes 1179656 | tf_op jit(solution)/shard_map/ppermute | solution.py:22
  55.4 20.6 %collective-permute-start.5 = (f32[3,128,1,256]{1,2,3,0:T(1,128)S(1)}, f32[3,128,1,256]{1,2,3,0:T(1,128)S(1)}, u32[]{:S(2)}, u32[]{:S(2)}) collective-permute-start(f32[3,128,1,256]{1,2,3,0:T(1,128)S(1)} %get-tuple-element.56), channel_id=1, source_target_pairs={{1,0},{2,1},{3,2},{4,3},{5,4},{6,5},{7,6},{0,7},{9,8},{10,9},{11,1... | collective-permute-start | bytes 1179656 | tf_op jit(solution)/shard_map/ppermute | solution.py:24
  79.9 16.5 %collective-permute-start.6 = (f32[3,128,1,256]{1,2,3,0:T(1,128)S(1)}, f32[3,128,1,256]{1,2,3,0:T(1,128)S(1)}, u32[]{:S(2)}, u32[]{:S(2)}) collective-permute-start(f32[3,128,1,256]{1,2,3,0:T(1,128)S(1)} %get-tuple-element.53), channel_id=1, source_target_pairs={{0,1},{1,2},{2,3},{3,4},{4,5},{5,6},{6,7},{7,0},{8,9},{9,10},{10,1... | collective-permute-start | bytes 1179656 | tf_op jit(solution)/shard_map/ppermute | solution.py:22
  79.9 20.1 %collective-permute-start.7 = (f32[3,128,1,256]{1,2,3,0:T(1,128)S(1)}, f32[3,128,1,256]{1,2,3,0:T(1,128)S(1)}, u32[]{:S(2)}, u32[]{:S(2)}) collective-permute-start(f32[3,128,1,256]{1,2,3,0:T(1,128)S(1)} %get-tuple-element.54), channel_id=1, source_target_pairs={{1,0},{2,1},{3,2},{4,3},{5,4},{6,5},{7,6},{0,7},{9,8},{10,9},{11,1... | collective-permute-start | bytes 1179656 | tf_op jit(solution)/shard_map/ppermute | solution.py:24
  107.1 16.5 %collective-permute-start.8 = (f32[3,128,1,256]{1,2,3,0:T(1,128)S(1)}, f32[3,128,1,256]{1,2,3,0:T(1,128)S(1)}, u32[]{:S(2)}, u32[]{:S(2)}) collective-permute-start(f32[3,128,1,256]{1,2,3,0:T(1,128)S(1)} %get-tuple-element.51), channel_id=1, source_target_pairs={{0,1},{1,2},{2,3},{3,4},{4,5},{5,6},{6,7},{7,0},{8,9},{9,10},{10,1... | collective-permute-start | bytes 1179656 | tf_op jit(solution)/shard_map/ppermute | solution.py:22
  107.2 18.7 %collective-permute-start.9 = (f32[3,128,1,256]{1,2,3,0:T(1,128)S(1)}, f32[3,128,1,256]{1,2,3,0:T(1,128)S(1)}, u32[]{:S(2)}, u32[]{:S(2)}) collective-permute-start(f32[3,128,1,256]{1,2,3,0:T(1,128)S(1)} %get-tuple-element.52), channel_id=1, source_target_pairs={{1,0},{2,1},{3,2},{4,3},{5,4},{6,5},{7,6},{0,7},{9,8},{10,9},{11,1... | collective-permute-start | bytes 1179656 | tf_op jit(solution)/shard_map/ppermute | solution.py:24
  129.7 15.8 %collective-permute-start.10 = (f32[3,128,1,256]{1,2,3,0:T(1,128)S(1)}, f32[3,128,1,256]{1,2,3,0:T(1,128)S(1)}, u32[]{:S(2)}, u32[]{:S(2)}) collective-permute-start(f32[3,128,1,256]{1,2,3,0:T(1,128)S(1)} %get-tuple-element.49), channel_id=1, source_target_pairs={{0,1},{1,2},{2,3},{3,4},{4,5},{5,6},{6,7},{7,0},{8,9},{9,10},{10,1... | collective-permute-start | bytes 1179656 | tf_op jit(solution)/shard_map/ppermute | solution.py:22
  130.0 20.2 %collective-permute-start.11 = (f32[3,128,1,256]{1,2,3,0:T(1,128)S(1)}, f32[3,128,1,256]{1,2,3,0:T(1,128)S(1)}, u32[]{:S(2)}, u32[]{:S(2)}) collective-permute-start(f32[3,128,1,256]{1,2,3,0:T(1,128)S(1)} %get-tuple-element.50), channel_id=1, source_target_pairs={{1,0},{2,1},{3,2},{4,3},{5,4},{6,5},{7,6},{0,7},{9,8},{10,9},{11,1... | collective-permute-start | bytes 1179656 | tf_op jit(solution)/shard_map/ppermute | solution.py:24
  157.3 17.2 %collective-permute-start.12 = (f32[3,128,1,256]{1,2,3,0:T(1,128)S(1)}, f32[3,128,1,256]{1,2,3,0:T(1,128)S(1)}, u32[]{:S(2)}, u32[]{:S(2)}) collective-permute-start(f32[3,128,1,256]{1,2,3,0:T(1,128)S(1)} %get-tuple-element.47), channel_id=1, source_target_pairs={{0,1},{1,2},{2,3},{3,4},{4,5},{5,6},{6,7},{7,0},{8,9},{9,10},{10,1... | collective-permute-start | bytes 1179656 | tf_op jit(solution)/shard_map/ppermute | solution.py:22
  157.3 19.8 %collective-permute-start.13 = (f32[3,128,1,256]{1,2,3,0:T(1,128)S(1)}, f32[3,128,1,256]{1,2,3,0:T(1,128)S(1)}, u32[]{:S(2)}, u32[]{:S(2)}) collective-permute-start(f32[3,128,1,256]{1,2,3,0:T(1,128)S(1)} %get-tuple-element.48), channel_id=1, source_target_pairs={{1,0},{2,1},{3,2},{4,3},{5,4},{6,5},{7,6},{0,7},{9,8},{10,9},{11,1... | collective-permute-start | bytes 1179656 | tf_op jit(solution)/shard_map/ppermute | solution.py:24
  181.0 16.5 %collective-permute-start.14 = (f32[3,128,1,256]{1,2,3,0:T(1,128)S(1)}, f32[3,128,1,256]{1,2,3,0:T(1,128)S(1)}, u32[]{:S(2)}, u32[]{:S(2)}) collective-permute-start(f32[3,128,1,256]{1,2,3,0:T(1,128)S(1)} %get-tuple-element.45), channel_id=1, source_target_pairs={{0,1},{1,2},{2,3},{3,4},{4,5},{5,6},{6,7},{7,0},{8,9},{9,10},{10,1... | collective-permute-start | bytes 1179656 | tf_op jit(solution)/shard_map/ppermute | solution.py:22
  181.1 20.5 %collective-permute-start.15 = (f32[3,128,1,256]{1,2,3,0:T(1,128)S(1)}, f32[3,128,1,256]{1,2,3,0:T(1,128)S(1)}, u32[]{:S(2)}, u32[]{:S(2)}) collective-permute-start(f32[3,128,1,256]{1,2,3,0:T(1,128)S(1)} %get-tuple-element.46), channel_id=1, source_target_pairs={{1,0},{2,1},{3,2},{4,3},{5,4},{6,5},{7,6},{0,7},{9,8},{10,9},{11,1... | collective-permute-start | bytes 1179656 | tf_op jit(solution)/shard_map/ppermute | solution.py:24
  209.8 3.8 copy-start.16
  209.8 40.7 %all-to-all-start = ((f32[3,128,8,256]{1,2,0,3:T(8,128)}), f32[3,128,8,256]{1,2,0,3:T(8,128)S(1)}, u32[]{:S(2)}, u32[]{:S(2)}) async-start(f32[3,128,8,256]{1,2,0,3:T(8,128)} %pad_maximum_fusion.27), calls=%async_computation | async-start | bytes 6291456 | tf_op jit(solution)/shard_map/all_to_all | solution.py:94
  213.6 3.5 copy-start.18
  213.7 3.5 copy-start.19
  259.2 3.4 copy-start.15
  259.2 3.4 copy-start.17
  262.8 14.0 %copy-start.3 = (f32[1,1,2,512,128]{3,4,2,1,0:T(8,128)}, f32[1,1,2,512,128]{3,4,2,1,0:T(8,128)S(1)}, u32[]{:S(2)}) copy-start(f32[1,1,2,512,128]{3,4,2,1,0:T(8,128)S(1)} %maximum_bitcast_fusion) | copy-start | bytes 1572868
  262.8 11.8 %collective-permute-start.17 = (f32[1,1,2,512,128]{3,4,2,1,0:T(8,128)S(1)}, f32[1,1,2,512,128]{3,4,2,1,0:T(8,128)S(1)}, u32[]{:S(2)}, u32[]{:S(2)}) collective-permute-start(f32[1,1,2,512,128]{3,4,2,1,0:T(8,128)S(1)} %maximum_bitcast_fusion), channel_id=1, source_target_pairs={{8,0},{16,8},{24,16},{0,24},{9,1},{17,9},{25,17},{1,25},{10,2},{18... | collective-permute-start | bytes 1572872 | tf_op jit(solution)/shard_map/ppermute | solution.py:24
  262.9 13.9 %collective-permute-start.16 = (f32[1,1,2,512,128]{3,4,2,1,0:T(8,128)S(1)}, f32[1,1,2,512,128]{3,4,2,1,0:T(8,128)S(1)}, u32[]{:S(2)}, u32[]{:S(2)}) collective-permute-start(f32[1,1,2,512,128]{3,4,2,1,0:T(8,128)S(1)} %maximum_bitcast_fusion), channel_id=1, source_target_pairs={{0,8},{8,16},{16,24},{24,0},{1,9},{9,17},{17,25},{25,1},{2,10},{10... | collective-permute-start | bytes 1572872 | tf_op jit(solution)/shard_map/ppermute | solution.py:22
  274.6 3.6 copy-start.11
  276.8 2.8 copy-start.13
  278.2 70.2 %collective-permute-start.19 = (f32[1,3,2,512,128]{3,4,2,1,0:T(8,128)}, f32[1,3,2,512,128]{3,4,2,1,0:T(8,128)}, u32[]{:S(2)}, u32[]{:S(2)}) collective-permute-start(f32[1,3,2,512,128]{3,4,2,1,0:T(8,128)} %pad_maximum_fusion.28), channel_id=1, source_target_pairs={{1,0},{2,1},{3,2},{4,3},{5,4},{6,5},{7,6},{0,7},{9,8},{10,9},{11,1... | collective-permute-start | bytes 4718600 | tf_op jit(solution)/shard_map/ppermute | solution.py:24
  279.6 68.8 %collective-permute-start.18 = (f32[1,3,2,512,128]{3,4,2,1,0:T(8,128)}, f32[1,3,2,512,128]{3,4,2,1,0:T(8,128)}, u32[]{:S(2)}, u32[]{:S(2)}) collective-permute-start(f32[1,3,2,512,128]{3,4,2,1,0:T(8,128)} %pad_maximum_fusion.28), channel_id=1, source_target_pairs={{0,1},{1,2},{2,3},{3,4},{4,5},{5,6},{6,7},{7,0},{8,9},{9,10},{10,1... | collective-permute-start | bytes 4718600 | tf_op jit(solution)/shard_map/ppermute | solution.py:22
  282.5 65.9 %copy-start.4 = (f32[1,1,2,512,128]{3,4,2,1,0:T(8,128)S(1)}, f32[1,1,2,512,128]{3,4,2,1,0:T(8,128)}, u32[]{:S(2)}) copy-start(f32[1,1,2,512,128]{3,4,2,1,0:T(8,128)} %copy-done.3) | copy-start | bytes 1572868
  282.5 65.9 %copy-start.12 = (f32[1,1,2,512,128]{3,4,2,1,0:T(8,128)S(1)}, f32[1,1,2,512,128]{3,4,2,1,0:T(8,128)}, u32[]{:S(2)}) copy-start(f32[1,1,2,512,128]{3,4,2,1,0:T(8,128)} %copy-done.11) | copy-start | bytes 1572868
  282.5 65.9 %copy-start.14 = (f32[1,1,2,512,128]{3,4,2,1,0:T(8,128)S(1)}, f32[1,1,2,512,128]{3,4,2,1,0:T(8,128)}, u32[]{:S(2)}) copy-start(f32[1,1,2,512,128]{3,4,2,1,0:T(8,128)} %copy-done.13) | copy-start | bytes 1572868
  362.9 1.0 copy-start.5
  378.2 17.4 %copy-start.2 = (f32[512,512]{1,0:T(8,128)S(1)}, f32[512,512]{1,0:T(8,128)}, u32[]{:S(2)}) copy-start(f32[512,512]{1,0:T(8,128)} %cholesky.224) | copy-start | bytes 3145732
  378.2 17.4 %copy-start.6 = (f32[512,512]{1,0:T(8,128)S(1)}, f32[512,512]{1,0:T(8,128)}, u32[]{:S(2)}) copy-start(f32[512,512]{1,0:T(8,128)} %copy-done.5) | copy-start | bytes 3145732
  457.1 51.7 %copy-start.8 = (f32[128,1152]{1,0:T(8,128)S(1)}, f32[128,1152]{1,0:T(8,128)}, u32[]{:S(2)}) copy-start(f32[128,1152]{1,0:T(8,128)} %copy.66) | copy-start | bytes 1769476
  508.1 2.1 copy-start.7
  510.1 1.5 copy-start.9
  517.1 2.0 copy-start.10
  519.0 4.8 copy-start.1
where the time goes:
time: 619 us; the launch traced here: 611 us
  waiting for transfers between devices  232 us (37%)
  other arithmetic  173 us (28%)
  local copies, waits for them, and re-layouts  82.7 us (13%)
  starting transfers between devices  46.8 us (8%)
  blocking collectives  40.7 us (7%)
  matrix products  31.9 us (5%)
    ppermute x10, waiting for transfers between devices, extended(): lax.ppermute(head, axis, [((i + 1) % count, i) for i in range(count)])  102 us
    ppermute x10, waiting for transfers between devices, extended(): lax.ppermute(tail, axis, [(i, (i + 1) % count) for i in range(count)])  96.8 us
    another operation x15, other arithmetic, analyse_tile(): factor = jnp.linalg.cholesky(gram)  79.6 us
    all_to_all x1, blocking collectives, local(): lax.all_to_all(updated, 'members', split_axis=1, concat_axis=3, tiled=True)  40.7 us
    another operation x3, other arithmetic, analyse_tile(): reduced = jax.scipy.linalg.cho_solve((factor, True), spread_all)  40.5 us
    ppermute x10, starting transfers between devices, extended(): lax.ppermute(head, axis, [((i + 1) % count, i) for i in range(count)])  38 us
    all_to_all x1, waiting for transfers between devices, local(): lax.all_to_all(state, 'members', split_axis=3, concat_axis=1, tiled=True)  33.3 us
    another operation x15, other arithmetic, local(): state = jnp.stack([eta_new, east, north])  18.8 us
  transfers between devices with their start and end apart: 21, of which 20 were waited for; matrix products, arithmetic and copies ran while one was open for 1% of the time, Pallas kernels for 0%

commit v1 on v0

--- a/solution.py
+++ b/solution.py
@@ -91,7 +91,12 @@
         east, north = momentum_update(padded[0], padded[1], padded[2])
         state = jnp.stack([eta_new, east, north])
     width = TILE_W
-    tiles = lax.all_to_all(state, "members", split_axis=3, concat_axis=1, tiled=True)
+    tiles = jnp.concatenate(
+        lax.all_to_all(
+            jnp.stack(jnp.split(state, lax.axis_size("members"), axis=3)), "members", 0, 0
+        ),
+        axis=1,
+    )
     count = tiles.shape[1]
     rows_here = tiles.shape[2]
     tile = tiles.reshape(3, count, rows_here * width)

time: 619 us -> 620 us (level)
  other arithmetic: 173 us -> 163 us
  local copies, waits for them, and re-layouts: 82.7 us -> 90.5 us
    another operation x12 -> x15, local copies, waits for them, and re-layouts: 10.6 us -> 22.7 us
    concatenate x10 -> x9, other arithmetic: 15 us -> 6.61 us  [extended(): jnp.concatenate([lax.ppermute(tail, axis, [(i, (i + 1) % count) for i in...]
    slice x30, local copies, waits for them, and re-layouts: 4.53 us -> 10.9 us  [centred_x(): return 0.5 * (jnp.roll(field, -1, axis=2) - jnp.roll(field, 1, axis=2))]
    unnamed x43 -> x41, local copies, waits for them, and re-layouts: 18.1 us -> 16.2 us
    another operation x15 -> x16, other arithmetic: 18.8 us -> 18.9 us  [local(): state = jnp.stack([eta_new, east, north])]
where the time goes in v1:
time: 620 us; the launch traced here: 611 us
  waiting for transfers between devices  235 us (38%)
  other arithmetic  163 us (26%)
  local copies, waits for them, and re-layouts  90.5 us (15%)
  starting transfers between devices  46.5 us (8%)
  blocking collectives  40.8 us (7%)
  matrix products  31.7 us (5%)
    ppermute x10, waiting for transfers between devices, extended(): lax.ppermute(head, axis, [((i + 1) % count, i) for i in range(count)])  105 us
    ppermute x10, waiting for transfers between devices, extended(): lax.ppermute(tail, axis, [(i, (i + 1) % count) for i in range(count)])  96.7 us
    another operation x15, other arithmetic, analyse_tile(): factor = jnp.linalg.cholesky(gram)  79.6 us
    all_to_all x1, blocking collectives, local(): lax.all_to_all(updated, 'members', split_axis=1, concat_axis=3, tiled=True)  40.8 us
    another operation x3, other arithmetic, analyse_tile(): reduced = jax.scipy.linalg.cho_solve((factor, True), spread_all)  40.4 us
    ppermute x10, starting transfers between devices, extended(): lax.ppermute(head, axis, [((i + 1) % count, i) for i in range(count)])  35.9 us
    all_to_all x1, waiting for transfers between devices, local(): lax.all_to_all(jnp.stack(jnp.split(state, lax.axis_size('members'), axis=...  33.3 us
    another operation x16, other arithmetic, local(): state = jnp.stack([eta_new, east, north])  18.9 us
  transfers between devices with their start and end apart: 21, of which 20 were waited for; matrix products, arithmetic and copies ran while one was open for 1% of the time, Pallas kernels for 0%

profile of v1, /device:TPU:0, one launch (start us, length us, event | category | flops | bytes accessed | tf_op | source)
XLA Modules:
  0.0 611.2 jit_solution(14675533651286494859)
XLA Ops:
  0.0 3.4 fusion.281
  3.5 3.0 collective-permute-start
  6.6 3.1 collective-permute-start.1
  10.3 13.0 %collective-permute-done = f32[3,128,1,256]{3,1,2,0:T(8,128)S(1)} collective-permute-done((f32[3,128,1,256]{3,1,2,0:T(8,128)S(1)}, f32[3,128,1,256]{3,1,2,0:T(8,128)S(1)}, u32[]{:S(2)}, u32[]{:S(2)}) %collective-permute-start) | collective-permute-done | bytes 393248 | tf_op jit(solution)/shard_map/ppermute | solution.py:22
  28.6 3.5 collective-permute-start.3
  32.2 12.4 %collective-permute-done.2 = f32[3,128,1,256]{3,1,2,0:T(8,128)S(1)} collective-permute-done((f32[3,128,1,256]{3,1,2,0:T(8,128)S(1)}, f32[3,128,1,256]{3,1,2,0:T(8,128)S(1)}, u32[]{:S(2)}, u32[]{:S(2)}) %collective-permute-start.2) | collective-permute-done | bytes 393248 | tf_op jit(solution)/shard_map/ppermute | solution.py:22
  54.7 4.7 collective-permute-start.5
  59.4 11.7 %collective-permute-done.4 = f32[3,128,1,256]{3,1,2,0:T(8,128)S(1)} collective-permute-done((f32[3,128,1,256]{3,1,2,0:T(8,128)S(1)}, f32[3,128,1,256]{3,1,2,0:T(8,128)S(1)}, u32[]{:S(2)}, u32[]{:S(2)}) %collective-permute-start.4) | collective-permute-done | bytes 393248 | tf_op jit(solution)/shard_map/ppermute | solution.py:22
  71.1 3.9 collective-permute-done.5
  77.5 4.9 collective-permute-start.7
  82.4 11.5 %collective-permute-done.6 = f32[3,128,1,256]{3,1,2,0:T(8,128)S(1)} collective-permute-done((f32[3,128,1,256]{3,1,2,0:T(8,128)S(1)}, f32[3,128,1,256]{3,1,2,0:T(8,128)S(1)}, u32[]{:S(2)}, u32[]{:S(2)}) %collective-permute-start.6) | collective-permute-done | bytes 393248 | tf_op jit(solution)/shard_map/ppermute | solution.py:22
  93.9 4.1 collective-permute-done.7
  105.1 4.7 collective-permute-start.9
  109.8 11.8 %collective-permute-done.8 = f32[3,128,1,256]{3,1,2,0:T(8,128)S(1)} collective-permute-done((f32[3,128,1,256]{3,1,2,0:T(8,128)S(1)}, f32[3,128,1,256]{3,1,2,0:T(8,128)S(1)}, u32[]{:S(2)}, u32[]{:S(2)}) %collective-permute-start.8) | collective-permute-done | bytes 393248 | tf_op jit(solution)/shard_map/ppermute | solution.py:22
  126.5 4.6 collective-permute-start.11
  131.2 11.0 %collective-permute-done.10 = f32[3,128,1,256]{3,1,2,0:T(8,128)S(1)} collective-permute-done((f32[3,128,1,256]{3,1,2,0:T(8,128)S(1)}, f32[3,128,1,256]{3,1,2,0:T(8,128)S(1)}, u32[]{:S(2)}, u32[]{:S(2)}) %collective-permute-start.10) | collective-permute-done | bytes 393248 | tf_op jit(solution)/shard_map/ppermute | solution.py:22
  152.2 5.1 collective-permute-start.13
  157.3 10.5 %collective-permute-done.12 = f32[3,128,1,256]{3,1,2,0:T(8,128)S(1)} collective-permute-done((f32[3,128,1,256]{3,1,2,0:T(8,128)S(1)}, f32[3,128,1,256]{3,1,2,0:T(8,128)S(1)}, u32[]{:S(2)}, u32[]{:S(2)}) %collective-permute-start.12) | collective-permute-done | bytes 393248 | tf_op jit(solution)/shard_map/ppermute | solution.py:22
  167.8 4.9 collective-permute-done.13
  175.2 4.7 collective-permute-start.15
  179.9 12.5 %collective-permute-done.14 = f32[3,128,1,256]{3,1,2,0:T(8,128)S(1)} collective-permute-done((f32[3,128,1,256]{3,1,2,0:T(8,128)S(1)}, f32[3,128,1,256]{3,1,2,0:T(8,128)S(1)}, u32[]{:S(2)}, u32[]{:S(2)}) %collective-permute-start.14) | collective-permute-done | bytes 393248 | tf_op jit(solution)/shard_map/ppermute | solution.py:22
  192.4 3.0 collective-permute-done.15
  206.6 6.1 copy.50
  212.7 3.8 all-to-all-start
  220.0 33.3 %all-to-all-done = f32[4,3,128,8,64]{2,4,3,1,0:T(8,128)S(1)} async-done(((f32[4,3,128,8,64]{2,4,3,1,0:T(8,128)}), f32[4,3,128,8,64]{2,4,3,1,0:T(8,128)S(1)}, u32[]{:S(2)}, u32[]{:S(2)}) %all-to-all-start) | async-done | bytes 3145760 | tf_op jit(solution)/shard_map/all_to_all | solution.py:95
  253.4 4.2 copy.51
  257.5 5.0 reshape_reshape.3
  262.6 3.4 fusion.315
  266.7 11.2 %collective-permute-done.17 = f32[1,1,2,512,128]{3,4,2,1,0:T(8,128)S(1)} collective-permute-done((f32[1,1,2,512,128]{3,4,2,1,0:T(8,128)S(1)}, f32[1,1,2,512,128]{3,4,2,1,0:T(8,128)S(1)}, u32[]{:S(2)}, u32[]{:S(2)}) %collective-permute-start.17) | collective-permute-done | bytes 524320 | tf_op jit(solution)/shard_map/ppermute | solution.py:24
  284.0 67.8 %collective-permute-done.19 = f32[1,3,2,512,128]{3,4,2,1,0:T(8,128)} collective-permute-done((f32[1,3,2,512,128]{3,4,2,1,0:T(8,128)}, f32[1,3,2,512,128]{3,4,2,1,0:T(8,128)}, u32[]{:S(2)}, u32[]{:S(2)}) %collective-permute-start.19) | collective-permute-done | bytes 1572896 | tf_op jit(solution)/shard_map/ppermute | solution.py:24
  354.5 5.7 convert_add_fusion
  369.9 11.7 %cholesky.104 = f32[128,128]{1,0:T(8,128)S(1)} custom-call(f32[128,128]{1,0:T(8,128)S(1)} %cholesky.266), custom_call_target="Cholesky" | custom-call | tf_op jit(solution)/shard_map/jit(cholesky)/cholesky | solution.py:79
  382.3 10.0 %custom-call.34 = f32[1,128,128]{1,2,0:T(8,128)S(1)} custom-call(f32[1,128,128]{2,1,0:T(8,128)S(1)} %get-tuple-element.144), custom_call_target="InvertDiagBlocksLowerTriangular" | custom-call | tf_op jit(solution)/shard_map/jit(cholesky)/cholesky | solution.py:79
  396.3 11.7 %cholesky.217 = f32[128,128]{1,0:T(8,128)S(1)} custom-call(f32[128,128]{1,0:T(8,128)S(1)} %cholesky.270), custom_call_target="Cholesky" | custom-call | tf_op jit(solution)/shard_map/jit(cholesky)/cholesky | solution.py:79
  408.8 9.8 %custom-call.35 = f32[1,128,128]{1,2,0:T(8,128)S(1)} custom-call(f32[1,128,128]{2,1,0:T(8,128)S(1)} %get-tuple-element.141), custom_call_target="InvertDiagBlocksLowerTriangular" | custom-call | tf_op jit(solution)/shard_map/jit(cholesky)/cholesky | solution.py:79
  419.3 11.7 %cholesky.238 = f32[128,128]{1,0:T(8,128)S(1)} custom-call(f32[128,128]{1,0:T(8,128)S(1)} %cholesky.275), custom_call_target="Cholesky" | custom-call | tf_op jit(solution)/shard_map/jit(cholesky)/cholesky | solution.py:79
  431.6 10.2 %custom-call.36 = f32[1,128,128]{1,2,0:T(8,128)S(1)} custom-call(f32[1,128,128]{2,1,0:T(8,128)S(1)} %get-tuple-element.138), custom_call_target="InvertDiagBlocksLowerTriangular" | custom-call | tf_op jit(solution)/shard_map/jit(cholesky)/cholesky | solution.py:79
  442.4 11.7 %cholesky.255 = f32[128,128]{1,0:T(8,128)S(1)} custom-call(f32[128,128]{1,0:T(8,128)S(1)} %convolution_subtract_fusion.8), custom_call_target="Cholesky" | custom-call | tf_op jit(solution)/shard_map/jit(cholesky)/cholesky | solution.py:79
  457.4 10.4 %while.1 = (s32[]{:T(128)}, f32[512,512]{1,0:T(8,128)S(1)}, s32[4,2]{0,1:T(2,128)S(1)}, f32[4,128,128]{2,1,0:T(8,128)}, s32[]{:T(128)}) while((s32[]{:T(128)}, f32[512,512]{1,0:T(8,128)S(1)}, s32[4,2]{0,1:T(2,128)S(1)}, f32[4,128,128]{2,1,0:T(8,128)}, s32[]{:T(128)}) %tuple.93), condition=%wide.while_cond, body=%wide.while_body.sunk | while | flops 2 | bytes 132205 | solution.py:80
  467.9 40.3 %custom-call.37 = f32[4,128,128]{1,2,0:T(8,128)S(1)} custom-call(f32[4,128,128]{2,1,0:T(8,128)} %get-tuple-element.12), custom_call_target="InvertDiagBlocksLowerTriangular" | custom-call | tf_op jit(solution)/shard_map/jit(_cho_solve)/triangular_solve | solution.py:80
  519.1 4.6 fusion.42
  523.8 5.4 bitcast_add_fusion
  529.1 4.2 copy.63
  533.4 7.0 %reshape.131 = f32[4,1,196608]{2,1,0:T(1,128)} reshape(f32[512,3,8,64]{3,2,1,0:T(8,128)} %bitcast.227) | data formatting | bytes 6291456
  540.4 40.8 %all_to_all.23 = f32[4,1,196608]{2,1,0:T(1,128)S(1)} all-to-all(f32[4,1,196608]{2,1,0:T(1,128)} %reshape.131), channel_id=1, replica_groups=mesh['members'=4,'space'=8] {'members'}, dimensions={0} | all-to-all | bytes 6291456 | tf_op jit(solution)/shard_map/all_to_all | solution.py:121
  581.8 10.6 %reduce.25 = f32[4,196608]{1,0:T(4,128)} reduce(f32[4,1,196608]{2,1,0:T(1,128)S(1)} %all_to_all.23, f32[]{:T(128)} %broadcast.379), dimensions={1}, to_apply=%all_to_all.17.reduce_sub_computation | reduce | bytes 6291460 | tf_op jit(solution)/shard_map/all_to_all | solution.py:121
  592.5 7.4 %reshape.132 = f32[512,3,8,64]{3,2,1,0:T(8,128)} reshape(f32[4,196608]{1,0:T(4,128)} %reduce.25) | data formatting | bytes 6291456
  599.9 6.1 copy.75
  (209 shorter events, 111.0 us)
Async XLA Ops:
  0.0 216.5 %copy-start = (f32[512,1,1,128]{3,2,1,0:T(1,128)S(1)}, f32[512,1,1,128]{3,2,1,0:T(1,128)}, u32[]{:S(2)}) copy-start(f32[512,1,1,128]{3,2,1,0:T(1,128)} %param.10) | copy-start | bytes 786436
  3.5 19.8 %collective-permute-start = (f32[3,128,1,256]{3,1,2,0:T(8,128)S(1)}, f32[3,128,1,256]{3,1,2,0:T(8,128)S(1)}, u32[]{:S(2)}, u32[]{:S(2)}) collective-permute-start(f32[3,128,1,256]{3,1,2,0:T(8,128)S(1)} %copy.77), channel_id=1, source_target_pairs={{0,1},{1,2},{2,3},{3,4},{4,5},{5,6},{6,7},{7,0},{8,9},{9,10},{10,1... | collective-permute-start | bytes 1179656 | tf_op jit(solution)/shard_map/ppermute | solution.py:22
  6.5 3.1 slice-start
  6.6 19.1 %collective-permute-start.1 = (f32[3,128,1,256]{3,1,2,0:T(8,128)S(1)}, f32[3,128,1,256]{3,1,2,0:T(8,128)S(1)}, u32[]{:S(2)}, u32[]{:S(2)}) collective-permute-start(f32[3,128,1,256]{3,1,2,0:T(8,128)S(1)} %copy.78), channel_id=1, source_target_pairs={{1,0},{2,1},{3,2},{4,3},{5,4},{6,5},{7,6},{0,7},{9,8},{10,9},{11,1... | collective-permute-start | bytes 1179656 | tf_op jit(solution)/shard_map/ppermute | solution.py:24
  9.7 13.7 %copy-start.2 = (f32[3,128,8,256]{3,2,1,0:T(8,128)S(1)}, f32[3,128,8,256]{3,2,1,0:T(8,128)}, u32[]{:S(2)}) copy-start(f32[3,128,8,256]{3,2,1,0:T(8,128)} %param.6) | copy-start | bytes 9437188
  27.4 17.2 %collective-permute-start.2 = (f32[3,128,1,256]{3,1,2,0:T(8,128)S(1)}, f32[3,128,1,256]{3,1,2,0:T(8,128)S(1)}, u32[]{:S(2)}, u32[]{:S(2)}) collective-permute-start(f32[3,128,1,256]{3,1,2,0:T(8,128)S(1)} %get-tuple-element.61), channel_id=1, source_target_pairs={{0,1},{1,2},{2,3},{3,4},{4,5},{5,6},{6,7},{7,0},{8,9},{9,10},{10,1... | collective-permute-start | bytes 1179656 | tf_op jit(solution)/shard_map/ppermute | solution.py:22
  28.6 18.9 %collective-permute-start.3 = (f32[3,128,1,256]{3,1,2,0:T(8,128)S(1)}, f32[3,128,1,256]{3,1,2,0:T(8,128)S(1)}, u32[]{:S(2)}, u32[]{:S(2)}) collective-permute-start(f32[3,128,1,256]{3,1,2,0:T(8,128)S(1)} %get-tuple-element.62), channel_id=1, source_target_pairs={{1,0},{2,1},{3,2},{4,3},{5,4},{6,5},{7,6},{0,7},{9,8},{10,9},{11,1... | collective-permute-start | bytes 1179656 | tf_op jit(solution)/shard_map/ppermute | solution.py:24
  54.6 16.5 %collective-permute-start.4 = (f32[3,128,1,256]{3,1,2,0:T(8,128)S(1)}, f32[3,128,1,256]{3,1,2,0:T(8,128)S(1)}, u32[]{:S(2)}, u32[]{:S(2)}) collective-permute-start(f32[3,128,1,256]{3,1,2,0:T(8,128)S(1)} %get-tuple-element.59), channel_id=1, source_target_pairs={{0,1},{1,2},{2,3},{3,4},{4,5},{5,6},{6,7},{7,0},{8,9},{9,10},{10,1... | collective-permute-start | bytes 1179656 | tf_op jit(solution)/shard_map/ppermute | solution.py:22
  54.7 20.3 %collective-permute-start.5 = (f32[3,128,1,256]{3,1,2,0:T(8,128)S(1)}, f32[3,128,1,256]{3,1,2,0:T(8,128)S(1)}, u32[]{:S(2)}, u32[]{:S(2)}) collective-permute-start(f32[3,128,1,256]{3,1,2,0:T(8,128)S(1)} %get-tuple-element.60), channel_id=1, source_target_pairs={{1,0},{2,1},{3,2},{4,3},{5,4},{6,5},{7,6},{0,7},{9,8},{10,9},{11,1... | collective-permute-start | bytes 1179656 | tf_op jit(solution)/shard_map/ppermute | solution.py:24
  77.5 16.5 %collective-permute-start.6 = (f32[3,128,1,256]{3,1,2,0:T(8,128)S(1)}, f32[3,128,1,256]{3,1,2,0:T(8,128)S(1)}, u32[]{:S(2)}, u32[]{:S(2)}) collective-permute-start(f32[3,128,1,256]{3,1,2,0:T(8,128)S(1)} %get-tuple-element.57), channel_id=1, source_target_pairs={{0,1},{1,2},{2,3},{3,4},{4,5},{5,6},{6,7},{7,0},{8,9},{9,10},{10,1... | collective-permute-start | bytes 1179656 | tf_op jit(solution)/shard_map/ppermute | solution.py:22
  77.5 20.5 %collective-permute-start.7 = (f32[3,128,1,256]{3,1,2,0:T(8,128)S(1)}, f32[3,128,1,256]{3,1,2,0:T(8,128)S(1)}, u32[]{:S(2)}, u32[]{:S(2)}) collective-permute-start(f32[3,128,1,256]{3,1,2,0:T(8,128)S(1)} %get-tuple-element.58), channel_id=1, source_target_pairs={{1,0},{2,1},{3,2},{4,3},{5,4},{6,5},{7,6},{0,7},{9,8},{10,9},{11,1... | collective-permute-start | bytes 1179656 | tf_op jit(solution)/shard_map/ppermute | solution.py:24
  105.1 16.5 %collective-permute-start.8 = (f32[3,128,1,256]{3,1,2,0:T(8,128)S(1)}, f32[3,128,1,256]{3,1,2,0:T(8,128)S(1)}, u32[]{:S(2)}, u32[]{:S(2)}) collective-permute-start(f32[3,128,1,256]{3,1,2,0:T(8,128)S(1)} %get-tuple-element.55), channel_id=1, source_target_pairs={{0,1},{1,2},{2,3},{3,4},{4,5},{5,6},{6,7},{7,0},{8,9},{9,10},{10,1... | collective-permute-start | bytes 1179656 | tf_op jit(solution)/shard_map/ppermute | solution.py:22
  105.1 18.9 %collective-permute-start.9 = (f32[3,128,1,256]{3,1,2,0:T(8,128)S(1)}, f32[3,128,1,256]{3,1,2,0:T(8,128)S(1)}, u32[]{:S(2)}, u32[]{:S(2)}) collective-permute-start(f32[3,128,1,256]{3,1,2,0:T(8,128)S(1)} %get-tuple-element.56), channel_id=1, source_target_pairs={{1,0},{2,1},{3,2},{4,3},{5,4},{6,5},{7,6},{0,7},{9,8},{10,9},{11,1... | collective-permute-start | bytes 1179656 | tf_op jit(solution)/shard_map/ppermute | solution.py:24
  126.4 15.8 %collective-permute-start.10 = (f32[3,128,1,256]{3,1,2,0:T(8,128)S(1)}, f32[3,128,1,256]{3,1,2,0:T(8,128)S(1)}, u32[]{:S(2)}, u32[]{:S(2)}) collective-permute-start(f32[3,128,1,256]{3,1,2,0:T(8,128)S(1)} %get-tuple-element.53), channel_id=1, source_target_pairs={{0,1},{1,2},{2,3},{3,4},{4,5},{5,6},{6,7},{7,0},{8,9},{9,10},{10,1... | collective-permute-start | bytes 1179656 | tf_op jit(solution)/shard_map/ppermute | solution.py:22
  126.5 18.6 %collective-permute-start.11 = (f32[3,128,1,256]{3,1,2,0:T(8,128)S(1)}, f32[3,128,1,256]{3,1,2,0:T(8,128)S(1)}, u32[]{:S(2)}, u32[]{:S(2)}) collective-permute-start(f32[3,128,1,256]{3,1,2,0:T(8,128)S(1)} %get-tuple-element.54), channel_id=1, source_target_pairs={{1,0},{2,1},{3,2},{4,3},{5,4},{6,5},{7,6},{0,7},{9,8},{10,9},{11,1... | collective-permute-start | bytes 1179656 | tf_op jit(solution)/shard_map/ppermute | solution.py:24
  152.2 15.6 %collective-permute-start.12 = (f32[3,128,1,256]{3,1,2,0:T(8,128)S(1)}, f32[3,128,1,256]{3,1,2,0:T(8,128)S(1)}, u32[]{:S(2)}, u32[]{:S(2)}) collective-permute-start(f32[3,128,1,256]{3,1,2,0:T(8,128)S(1)} %get-tuple-element.51), channel_id=1, source_target_pairs={{0,1},{1,2},{2,3},{3,4},{4,5},{5,6},{6,7},{7,0},{8,9},{9,10},{10,1... | collective-permute-start | bytes 1179656 | tf_op jit(solution)/shard_map/ppermute | solution.py:22
  152.2 20.4 %collective-permute-start.13 = (f32[3,128,1,256]{3,1,2,0:T(8,128)S(1)}, f32[3,128,1,256]{3,1,2,0:T(8,128)S(1)}, u32[]{:S(2)}, u32[]{:S(2)}) collective-permute-start(f32[3,128,1,256]{3,1,2,0:T(8,128)S(1)} %get-tuple-element.52), channel_id=1, source_target_pairs={{1,0},{2,1},{3,2},{4,3},{5,4},{6,5},{7,6},{0,7},{9,8},{10,9},{11,1... | collective-permute-start | bytes 1179656 | tf_op jit(solution)/shard_map/ppermute | solution.py:24
  175.1 17.3 %collective-permute-start.14 = (f32[3,128,1,256]{3,1,2,0:T(8,128)S(1)}, f32[3,128,1,256]{3,1,2,0:T(8,128)S(1)}, u32[]{:S(2)}, u32[]{:S(2)}) collective-permute-start(f32[3,128,1,256]{3,1,2,0:T(8,128)S(1)} %get-tuple-element.49), channel_id=1, source_target_pairs={{0,1},{1,2},{2,3},{3,4},{4,5},{5,6},{6,7},{7,0},{8,9},{9,10},{10,1... | collective-permute-start | bytes 1179656 | tf_op jit(solution)/shard_map/ppermute | solution.py:22
  175.2 20.3 %collective-permute-start.15 = (f32[3,128,1,256]{3,1,2,0:T(8,128)S(1)}, f32[3,128,1,256]{3,1,2,0:T(8,128)S(1)}, u32[]{:S(2)}, u32[]{:S(2)}) collective-permute-start(f32[3,128,1,256]{3,1,2,0:T(8,128)S(1)} %get-tuple-element.50), channel_id=1, source_target_pairs={{1,0},{2,1},{3,2},{4,3},{5,4},{6,5},{7,6},{0,7},{9,8},{10,9},{11,1... | collective-permute-start | bytes 1179656 | tf_op jit(solution)/shard_map/ppermute | solution.py:24
  212.7 3.8 copy-start.13
  212.7 40.7 %all-to-all-start = ((f32[4,3,128,8,64]{2,4,3,1,0:T(8,128)}), f32[4,3,128,8,64]{2,4,3,1,0:T(8,128)S(1)}, u32[]{:S(2)}, u32[]{:S(2)}) async-start(f32[4,3,128,8,64]{2,4,3,1,0:T(8,128)} %copy.50), calls=%async_computation | async-start | bytes 6291456 | tf_op jit(solution)/shard_map/all_to_all | solution.py:95
  216.6 3.5 copy-start.15
  216.6 3.4 copy-start.16
  262.6 3.4 copy-start.12
  262.6 3.4 copy-start.14
  266.2 15.3 %copy-start.3 = (f32[1,1,2,512,128]{3,4,2,1,0:T(8,128)}, f32[1,1,2,512,128]{3,4,2,1,0:T(8,128)S(1)}, u32[]{:S(2)}) copy-start(f32[1,1,2,512,128]{3,4,2,1,0:T(8,128)S(1)} %maximum_bitcast_fusion) | copy-start | bytes 1572868
  266.2 11.8 %collective-permute-start.17 = (f32[1,1,2,512,128]{3,4,2,1,0:T(8,128)S(1)}, f32[1,1,2,512,128]{3,4,2,1,0:T(8,128)S(1)}, u32[]{:S(2)}, u32[]{:S(2)}) collective-permute-start(f32[1,1,2,512,128]{3,4,2,1,0:T(8,128)S(1)} %maximum_bitcast_fusion), channel_id=1, source_target_pairs={{8,0},{16,8},{24,16},{0,24},{9,1},{17,9},{25,17},{1,25},{10,2},{18... | collective-permute-start | bytes 1572872 | tf_op jit(solution)/shard_map/ppermute | solution.py:24
  266.3 13.9 %collective-permute-start.16 = (f32[1,1,2,512,128]{3,4,2,1,0:T(8,128)S(1)}, f32[1,1,2,512,128]{3,4,2,1,0:T(8,128)S(1)}, u32[]{:S(2)}, u32[]{:S(2)}) collective-permute-start(f32[1,1,2,512,128]{3,4,2,1,0:T(8,128)S(1)} %maximum_bitcast_fusion), channel_id=1, source_target_pairs={{0,8},{8,16},{16,24},{24,0},{1,9},{9,17},{17,25},{25,1},{2,10},{10... | collective-permute-start | bytes 1572872 | tf_op jit(solution)/shard_map/ppermute | solution.py:22
  278.0 3.5 copy-start.10
  280.2 1.3 copy-start.11
  281.5 70.2 %collective-permute-start.19 = (f32[1,3,2,512,128]{3,4,2,1,0:T(8,128)}, f32[1,3,2,512,128]{3,4,2,1,0:T(8,128)}, u32[]{:S(2)}, u32[]{:S(2)}) collective-permute-start(f32[1,3,2,512,128]{3,4,2,1,0:T(8,128)} %pad_maximum_fusion.28), channel_id=1, source_target_pairs={{1,0},{2,1},{3,2},{4,3},{5,4},{6,5},{7,6},{0,7},{9,8},{10,9},{11,1... | collective-permute-start | bytes 4718600 | tf_op jit(solution)/shard_map/ppermute | solution.py:24
  282.0 69.8 %collective-permute-start.18 = (f32[1,3,2,512,128]{3,4,2,1,0:T(8,128)}, f32[1,3,2,512,128]{3,4,2,1,0:T(8,128)}, u32[]{:S(2)}, u32[]{:S(2)}) collective-permute-start(f32[1,3,2,512,128]{3,4,2,1,0:T(8,128)} %pad_maximum_fusion.28), channel_id=1, source_target_pairs={{0,1},{1,2},{2,3},{3,4},{4,5},{5,6},{6,7},{7,0},{8,9},{9,10},{10,1... | collective-permute-start | bytes 4718600 | tf_op jit(solution)/shard_map/ppermute | solution.py:22
  366.2 2.2 copy-start.4
  369.9 24.6 %copy-start.5 = (f32[128,3,3,128]{0,3,2,1:T(8,128)S(1)}, f32[128,3,3,128]{0,3,2,1:T(8,128)}, u32[]{:S(2)}) copy-start(f32[128,3,3,128]{0,3,2,1:T(8,128)} %get-tuple-element.68) | copy-start | bytes 1769476
  457.4 51.5 %copy-start.7 = (f32[128,1152]{1,0:T(8,128)S(1)}, f32[128,1152]{1,0:T(8,128)}, u32[]{:S(2)}) copy-start(f32[128,1152]{1,0:T(8,128)} %copy.58) | copy-start | bytes 1769476
  508.9 1.3 copy-start.6
  510.2 1.5 copy-start.8
  517.2 2.0 copy-start.9
  519.1 4.6 copy-start.1
